TPU v7x, 128 devices: a whole 4x4x4 slice. The times are simulated.
128 devices in a mesh: rec: 4 (over z), tm: 32 (over x, y, core).
Axes of the slice: x: 4, y: 4, z: 4, core: 2. Of those that a mesh axis runs over, the one named last changes fastest.
Arguments:
- mel_frames: bfloat16 [4, 65536, 80], P('rec', 'tm'), may hold values from -6 to 6
- lengths: int32 [4, 4], P('rec'), may hold values from 1 to 32768, 65536 in all within a row
- w_first: float32 [3, 3, 256], replicated, may hold values from -2 to 2
- w_second: bfloat16 [2304, 256], P(('rec', 'tm')), may hold values from -0.125 to 0.125
- w_proj: bfloat16 [5120, 1024], P(('rec', 'tm')), may hold values from -0.078125 to 0.078125
- gain_attn: float32 [1024], replicated, may hold values from 0.5 to 1.5
- w_qkv: bfloat16 [1024, 3072], P(('rec', 'tm')), may hold values from -2 to 2
- w_out: bfloat16 [1024, 1024], P(('rec', 'tm')), may hold values from -0.1875 to 0.1875
- gain_conv: float32 [1024], replicated, may hold values from 0.5 to 1.5
- w_point_in: bfloat16 [1024, 2048], P(('rec', 'tm')), may hold values from -0.1875 to 0.1875
- w_depth: float32 [9, 1024], replicated, may hold values from -6 to 6
- w_point_out: bfloat16 [1024, 1024], P(('rec', 'tm')), may hold values from -0.375 to 0.375
- gain_out: float32 [1024], replicated, may hold values from 0.5 to 1.5
Outputs:
- encoded: bfloat16 [4, 16384, 1024], P('rec', 'tm')
Inputs may be any that keep to these rules, and one draw needn't show every extreme that they name: Each group's 4 lengths sum to 65536, and the largest of them is 32768.
All inputs are finite; a program needn't handle non-finite values.
Results may differ from a plain program's by a relative error of at most 0.024.
The roundings to bfloat16 on the way count: a program that leaves them out, or rounds other values in their place, can miss the bound.
Values may be sent and summed in bfloat16 or wider, within the bound.
A program may use at most 128 MiB of HBM per device.

v0:
```python
import jax
import jax.numpy as jnp
from jax import lax
from jax.sharding import PartitionSpec as P

WIDTH = 1024
HEADS = 8
KERNEL = 9
WINDOW = 128
CONV_BLOCK = 64
HEAD_DIM = 128
NORM_EPSILON = 1e-05


def passed_along(block, axis, distance):
    devices = range(lax.axis_size(axis))
    route = [(i - distance, i) for i in devices if i - distance in devices]
    return lax.ppermute(block, axis, route)


def with_halo(block, sides, width):
    for axis, dim in sides:
        count = lax.axis_size(axis)
        forward = [(i, i + 1) for i in range(count - 1)]
        backward = [(target, source) for source, target in forward]
        low = lax.ppermute(
            lax.slice_in_dim(block, block.shape[dim] - width, None, axis=dim), axis, forward
        )
        high = lax.ppermute(lax.slice_in_dim(block, 0, width, axis=dim), axis, backward)
        block = jnp.concatenate([low, block, high], axis=dim)
    return block


def layer_norm(values, gain):
    row_mean = jnp.mean(values, axis=-1, keepdims=True)
    centred = values - row_mean
    variance = jnp.mean(centred * centred, axis=-1, keepdims=True)
    return centred * lax.rsqrt(variance + NORM_EPSILON) * gain


def segment_ids(positions, bounds, limit):
    counted = jnp.sum((positions[:, None] >= bounds[None, :-1]).astype(jnp.int32), axis=1)
    inside = (positions >= 0) & (positions < limit)
    return jnp.where(inside, counted, -1)


def conv_first(window, seg_rows, w_first):
    frame_count = (window.shape[0] - 1) // 2
    bins = window.shape[1]
    padded = jnp.pad(window.astype(jnp.float32), ((0, 0), (1, 1)))
    centre = seg_rows[1 : 2 * frame_count : 2]
    total = jnp.zeros((frame_count, bins // 2, w_first.shape[-1]), jnp.float32)
    for step_t in range(3):
        taken = padded[step_t : step_t + 2 * frame_count - 1 : 2]
        same_seg = (seg_rows[step_t : step_t + 2 * frame_count - 1 : 2] == centre).astype(
            jnp.float32
        )
        taken = taken * same_seg[:, None]
        for step_f in range(3):
            columns = taken[:, step_f : step_f + bins - 1 : 2]
            total = total + columns[:, :, None] * w_first[step_t, step_f][None, None, :]
    return jnp.maximum(total, 0.0).astype(jnp.bfloat16)


def conv_second(first, seg_first, w_second):
    frame_count = (first.shape[0] - 1) // 2
    channels = first.shape[2]
    quarter = first.shape[1] // 2
    padded = jnp.pad(first, ((0, 0), (1, 1), (0, 0)))
    centre = seg_first[1 : 2 * frame_count : 2]
    total = jnp.zeros((frame_count * quarter, w_second.shape[1]), jnp.float32)
    for step_t in range(3):
        taken = padded[step_t : step_t + 2 * frame_count - 1 : 2]
        same_seg = (seg_first[step_t : step_t + 2 * frame_count - 1 : 2] == centre).astype(
            jnp.bfloat16
        )
        taken = taken * same_seg[:, None, None]
        for step_f in range(3):
            columns = taken[:, step_f : step_f + 2 * quarter - 1 : 2].reshape(
                frame_count * quarter, channels
            )
            offset = (step_t * 3 + step_f) * channels
            total = total + jnp.dot(
                columns, w_second[offset : offset + channels], preferred_element_type=jnp.float32
            )
    return jnp.maximum(total, 0.0).astype(jnp.bfloat16).reshape(frame_count, quarter * channels)


def attend_block(q_block, kv_block, q_seg, k_seg):
    row_count = q_block.shape[0]
    span = kv_block.shape[0]
    reach = (span - row_count) // 2
    offsets = (
        jnp.arange(span, dtype=jnp.int32)[None, :]
        - jnp.arange(row_count, dtype=jnp.int32)[:, None]
        - reach
    )
    allowed = (jnp.abs(offsets) <= reach) & (k_seg[None, :] == q_seg[:, None])

    def one_head(head):
        start = head * HEAD_DIM
        q_head = lax.dynamic_slice_in_dim(q_block, start, HEAD_DIM, 1)
        k_head = lax.dynamic_slice_in_dim(kv_block, start, HEAD_DIM, 1)
        v_head = lax.dynamic_slice_in_dim(kv_block, WIDTH + start, HEAD_DIM, 1)
        scores = lax.dot_general(
            q_head, k_head, (((1,), (1,)), ((), ())), preferred_element_type=jnp.float32
        ) * HEAD_DIM ** (-0.5)
        scores = jnp.where(allowed, scores, -1e30)
        row_max = jnp.max(scores, axis=-1, keepdims=True)
        exped = jnp.where(allowed, jnp.exp(scores - row_max), 0.0)
        probabilities = (exped / jnp.sum(exped, axis=-1, keepdims=True)).astype(jnp.bfloat16)
        return jnp.dot(probabilities, v_head, preferred_element_type=jnp.float32).astype(
            jnp.bfloat16
        )

    per_head = lax.map(one_head, jnp.arange(HEADS, dtype=jnp.int32))
    return jnp.transpose(per_head, (1, 0, 2)).reshape(row_count, WIDTH)


def depthwise(gated_ext, seg_ext, seg_mid, w_depth):
    length = seg_mid.shape[0]
    total = jnp.zeros((length, gated_ext.shape[1]), jnp.float32)
    for tap_index in range(w_depth.shape[0]):
        same_seg = (seg_ext[tap_index : tap_index + length] == seg_mid).astype(jnp.float32)
        total = (
            total
            + gated_ext[tap_index : tap_index + length].astype(jnp.float32)
            * w_depth[tap_index][None, :]
            * same_seg[:, None]
        )
    return jax.nn.silu(total).astype(jnp.bfloat16)


def add_product(inputs, piece):
    return jnp.dot(inputs, piece, preferred_element_type=jnp.float32)


def on_device(
    mel_frames,
    lengths,
    w_first,
    w_second,
    w_proj,
    gain_attn,
    w_qkv,
    w_out,
    gain_conv,
    w_point_in,
    w_depth,
    w_point_out,
    gain_out,
):
    frames_dev = mel_frames.shape[1]
    tokens_dev = frames_dev // 4
    shards = lax.axis_size("tm")
    index = lax.axis_index("tm")
    frames_all = frames_dev * shards
    bounds = jnp.cumsum(lengths[0])
    local_mel = mel_frames[0]
    first_base = index * frames_dev
    second_full = lax.all_gather(w_second, ("rec", "tm"), axis=0, tiled=True)
    block_count = tokens_dev // CONV_BLOCK
    mel_edge = passed_along(local_mel[frames_dev - 3 :], "tm", 1)
    extended = jnp.concatenate([mel_edge, local_mel], axis=0)

    def sub_block(block):
        start = block * CONV_BLOCK
        window = lax.dynamic_slice_in_dim(extended, 4 * start, 4 * CONV_BLOCK + 3, 0)
        positions = first_base + 4 * start - 3 + jnp.arange(4 * CONV_BLOCK + 3, dtype=jnp.int32)
        seg_rows = segment_ids(positions, bounds, frames_all)
        first = conv_first(window, seg_rows, w_first)
        return conv_second(first, seg_rows[1::2], second_full)

    sub = lax.map(sub_block, jnp.arange(block_count, dtype=jnp.int32))
    sub = sub.reshape(tokens_dev, sub.shape[-1])
    hidden = add_product(sub, lax.all_gather(w_proj, ("rec", "tm"), axis=0, tiled=True))
    token_pos = index * tokens_dev + jnp.arange(tokens_dev, dtype=jnp.int32)
    token_seg = segment_ids(4 * token_pos, bounds, frames_all)
    key_pos = index * tokens_dev - WINDOW + jnp.arange(tokens_dev + 2 * WINDOW, dtype=jnp.int32)
    key_seg = segment_ids(4 * key_pos, bounds, frames_all)
    normed = layer_norm(hidden, gain_attn).astype(jnp.bfloat16)
    mixed = add_product(normed, lax.all_gather(w_qkv, ("rec", "tm"), axis=0, tiled=True)).astype(
        jnp.bfloat16
    )
    query = mixed[:, :WIDTH]
    keyval = with_halo(mixed[:, WIDTH:], (("tm", 0),), WINDOW)
    block_rows = min(512, tokens_dev)
    block = 0
    start = block * block_rows
    pieces = attend_block(query, keyval, token_seg, key_seg)
    attn_out = add_product(pieces, lax.all_gather(w_out, ("rec", "tm"), axis=0, tiled=True))
    attended = hidden + attn_out
    normed_conv = layer_norm(attended, gain_conv).astype(jnp.bfloat16)
    upward = add_product(normed_conv, lax.all_gather(w_point_in, ("rec", "tm"), axis=0, tiled=True))
    gated = (upward[:, :WIDTH] * jax.nn.sigmoid(upward[:, WIDTH:])).astype(jnp.bfloat16)
    reach = KERNEL // 2
    gated_ext = with_halo(gated, (("tm", 0),), KERNEL // 2)
    depth_pos = index * tokens_dev - reach + jnp.arange(tokens_dev + 2 * reach, dtype=jnp.int32)
    seg_ext = segment_ids(4 * depth_pos, bounds, frames_all)
    acted = depthwise(gated_ext, seg_ext, token_seg, w_depth)
    conv_out = add_product(acted, lax.all_gather(w_point_out, ("rec", "tm"), axis=0, tiled=True))
    combined = attended + conv_out
    return layer_norm(combined, gain_out).astype(jnp.bfloat16)[None]


def solution(mesh):
    placed = (
        P("rec", "tm", None),
        P("rec", None),
        P(),
        P(("rec", "tm"), None),
        P(("rec", "tm"), None),
        P(),
        P(("rec", "tm"), None),
        P(("rec", "tm"), None),
        P(),
        P(("rec", "tm"), None),
        P(),
        P(("rec", "tm"), None),
        P(),
    )
    return jax.shard_map(
        on_device, mesh=mesh, in_specs=placed, out_specs=P("rec", "tm", None), check_vma=False
    )
```

profile of v0, /device:TPU:25, one launch (start us, length us, event | category | flops | bytes accessed | tf_op | source)
XLA Modules:
  0.0 880.1 jit_solution(9001724628954924536)
XLA Ops:
  18.9 56.1 %all-gather.18.cloned.1.call-done = bf16[128,18,256]{2,1,0:T(8,128)(2,1)} async-done(((bf16[1,18,256]{2,1,0:T(8,128)(2,1)}), bf16[128,18,256]{2,1,0:T(8,128)(2,1)}) %all-gather.18.cloned.1.call-update) | async-done | bytes 1179664 | tf_op jit(solution)/shard_map/all_gather | solution.py:161
  78.8 684.2 %while.25 = (s32[]{:T(128)}, bf16[8,64,5120]{2,1,0:T(8,128)(2,1)}, s32[8]{0:T(128)}, bf16[2051,80]{1,0:T(8,128)(2,1)}, s32[]{:T(128)}, /*index=5*/s32[4]{0:T(128...) while((s32[]{:T(128)}, bf16[8,64,5120]{2,1,0:T(8,128)(2,1)}, ...), condition=%wide.region_3.4_spmd, body=%wide.region_1.3_spmd.sunk | while | flops 1543876352 | bytes 92566552 | solution.py:174
  90.5 7.7 maximum_convert_fusion.2
  101.9 6.9 slice.735
  114.6 4.9 slice.737
  123.2 4.8 slice.738
  135.1 4.9 slice.740
  155.5 4.9 slice.743
  176.2 7.7 maximum_convert_fusion.2
  187.6 6.9 slice.735
  200.4 4.9 slice.737
  220.8 4.9 slice.740
  241.1 4.9 slice.743
  261.8 7.7 maximum_convert_fusion.2
  273.2 6.9 slice.735
  286.0 4.9 slice.737
  306.3 4.9 slice.740
  326.6 4.9 slice.743
  347.3 7.7 maximum_convert_fusion.2
  358.7 6.9 slice.735
  371.5 4.9 slice.737
  391.8 4.9 slice.740
  412.1 4.9 slice.743
  432.8 7.7 maximum_convert_fusion.2
  444.2 6.9 slice.735
  457.0 4.9 slice.737
  477.3 4.9 slice.740
  497.6 4.9 slice.743
  518.3 7.7 maximum_convert_fusion.2
  529.7 6.9 slice.735
  542.4 4.9 slice.737
  562.7 4.9 slice.740
  583.0 4.9 slice.743
  603.7 7.7 maximum_convert_fusion.2
  615.1 6.9 slice.735
  627.9 4.9 slice.737
  648.2 4.9 slice.740
  668.5 4.9 slice.743
  689.2 7.7 maximum_convert_fusion.2
  700.6 6.9 slice.735
  713.3 4.9 slice.737
  733.6 4.9 slice.740
  754.0 4.9 slice.743
  763.0 10.0 %fusion.62 = (f32[512]{0:T(512)S(1)}, f32[512,1024]{1,0:T(8,128)S(1)}) fusion(bf16[512,5120]{1,0:T(8,128)(2,1)} %bitcast.117, bf16[5120,1024]{1,0:T(8,128)(2,1)} %all-gather.8.cloned.1.call-done), kind=kOutput, calls=%fused_computation.140 | convolution fusion | flops 5369232896 | bytes 17827840 | tf_op jit(solution)/shard_map/dot_general | solution.py:135
  773.7 6.6 convolution_convert_fusion.1
  790.5 6.5 collective-permute-done.2
  798.8 47.7 %while.26 = (s32[]{:T(128)}, bf16[8,512,128]{1,2,0:T(8,128)(2,1)}, s32[8]{0:T(128)S(1)}, bf16[512,1024]{1,0:T(8,128)(2,1)S(1)}, bf16[768,2048]{1,0:T(8,128)(2,1)...) while((s32[]{:T(128)}, bf16[8,512,128]{1,2,0:T(8,128)(2,1)}, ...), condition=%wide.region_11.12_spmd.clone, body=%wide.region_8.11_spmd.clone.sunk | while | flops 212401152 | bytes 5925630 | solution.py:116
  865.3 6.0 fusion.64
  (655 shorter events, 529.8 us)
Async XLA Ops:
  6.5 68.5 %all-gather.18.cloned.1.call-start = ((), (), s32[]{:S(2)}) async-start(), calls=%async_computation.5 | async-start | bytes 1585152 | tf_op jit(solution)/shard_map/all_gather | solution.py:161
  7.3 755.7 %all-gather.8.cloned.1.call-start = ((), (), s32[]{:S(2)}) async-start(), calls=%async_computation | async-start | bytes 10567680 | tf_op jit(solution)/shard_map/all_gather | solution.py:176
  8.0 765.4 %all-gather.10.cloned.1.call-start = ((), (), s32[]{:S(2)}) async-start(), calls=%async_computation.1 | async-start | bytes 6340608 | tf_op jit(solution)/shard_map/all_gather | solution.py:182
  8.7 837.7 %all-gather.12.cloned.1.call-start = ((), (), s32[]{:S(2)}) async-start(), calls=%async_computation.2 | async-start | bytes 2113536 | tf_op jit(solution)/shard_map/all_gather | solution.py:191
  9.3 841.5 %all-gather.14.cloned.1.call-start = ((), (), s32[]{:S(2)}) async-start(), calls=%async_computation.3 | async-start | bytes 4227072 | tf_op jit(solution)/shard_map/all_gather | solution.py:194
  9.9 851.0 %all-gather.16.cloned.1.call-start = ((), (), s32[]{:S(2)}) async-start(), calls=%async_computation.4 | async-start | bytes 2113536 | tf_op jit(solution)/shard_map/all_gather | solution.py:201
  11.2 67.6 %copy-start.7 = (f32[3,3,256]{2,1,0:T(4,128)S(1)}, f32[3,3,256]{2,1,0:T(4,128)}, u32[]{:S(2)}) copy-start(f32[3,3,256]{2,1,0:T(4,128)} %param.19) | copy-start | bytes 27652
  11.2 6.7 collective-permute-start
  16.6 62.2 %copy-start.11 = (s32[3]{0:T(128)}, s32[3]{0:T(128)S(1)}, u32[]{:S(2)}) copy-start(s32[3]{0:T(128)S(1)} %slice_bitcast_fusion.1) | copy-start | bytes 40
  119.5 3.7 copy-start.1
  123.2 6.2 copy-start.4
  140.1 3.8 copy-start
  143.8 6.0 copy-start.3
  205.3 3.8 copy-start.1
  209.1 6.0 copy-start.4
  225.7 3.7 copy-start
  229.4 6.0 copy-start.3
  290.9 3.7 copy-start.1
  294.6 6.0 copy-start.4
  311.2 3.7 copy-start
  314.9 6.0 copy-start.3
  380.0 6.0 copy-start.4
  396.7 3.7 copy-start
  400.4 6.0 copy-start.3
  465.5 6.0 copy-start.4
  482.2 3.7 copy-start
  485.9 6.0 copy-start.3
  547.3 3.7 copy-start.1
  551.0 6.0 copy-start.4
  567.6 3.7 copy-start
  571.3 6.0 copy-start.3
  636.4 6.0 copy-start.4
  653.1 3.7 copy-start
  656.8 6.0 copy-start.3
  721.9 6.0 copy-start.4
  738.6 3.7 copy-start
  742.3 6.0 copy-start.3
  773.0 7.3 copy-start.6
  780.3 6.4 copy-start.5
  780.3 6.0 copy-start.10
  780.3 6.0 copy-start.12
  780.3 6.1 copy-start.8
  780.3 6.1 copy-start.9
  780.4 10.1 %collective-permute-start.1 = (bf16[128,2048]{1,0:T(8,128)(2,1)S(1)}, bf16[128,2048]{1,0:T(8,128)(2,1)S(1)}, u32[]{:S(2)}, u32[]{:S(2)}) collective-permute-start(bf16[128,2048]{1,0:T(8,128)(2,1)S(1)} %get-tuple-element.258), channel_id=1, source_target_pairs={{0,1},{1,2},{2,3},{3,4},{4,5},{5,6},{6,7},{7,8},{8,9},{9,10},{10,1... | collective-permute-start | bytes 1572872 | tf_op jit(solution)/shard_map/ppermute | solution.py:26
  784.4 12.6 %collective-permute-start.2 = (bf16[128,2048]{1,0:T(8,128)(2,1)S(1)}, bf16[128,2048]{1,0:T(8,128)(2,1)S(1)}, u32[]{:S(2)}, u32[]{:S(2)}) collective-permute-start(bf16[128,2048]{1,0:T(8,128)(2,1)S(1)} %get-tuple-element.259), channel_id=1, source_target_pairs={{1,0},{2,1},{3,2},{4,3},{5,4},{6,5},{7,6},{8,7},{9,8},{10,9},{11,1... | collective-permute-start | bytes 1572872 | tf_op jit(solution)/shard_map/ppermute | solution.py:29
  786.7 12.1 %slice-start = ((bf16[512,3072]{1,0:T(8,128)(2,1)}), bf16[512,1024]{1,0:T(8,128)(2,1)S(1)}, s32[]{:S(2)}) async-start(bf16[512,3072]{1,0:T(8,128)(2,1)} %copy-done.5), calls=%async_computation.6 | async-start | bytes 2097152 | tf_op jit(solution)/shard_map/slice | solution.py:185
  856.3 4.7 collective-permute-start.3
  858.2 7.1 collective-permute-start.4
  (15 other events, 37.1 us)
Sparse Core Ops, SparseCore 0:
  10.2 64.8 all-gather.17
  78.2 70.0 all-gather.7
  151.5 65.5 all-gather.9
  220.0 62.7 all-gather.11
  285.8 64.3 all-gather.13
  353.1 62.7 all-gather.15
where the time goes:
time: 886 us; the launch traced here: 880 us
  local copies, waits for them, and re-layouts  458 us (52%)
  matrix products  202 us (23%)
  other arithmetic  106 us (12%)
  waiting for transfers between devices  74 us (8%)
  starting transfers between devices  14 us (2%)
  between operations  13.8 us (2%)
  loops' own time  12.6 us (1%)
    slice x72, local copies, waits for them, and re-layouts, conv_second(): taken[:, step_f:step_f + 2 * quarter - 1:2]  284 us
    dot_general x72, matrix products, conv_second(): jnp.dot(columns, w_second[offset:offset + channels], preferred_element_ty...  145 us
    convert_element_type x8, other arithmetic, conv_first(): return jnp.maximum(total, 0.0).astype(jnp.bfloat16)  61.5 us
    slice x72, local copies, waits for them, and re-layouts, conv_first(): columns = taken[:, step_f:step_f + bins - 1:2]  57.2 us
    reshape x72, local copies, waits for them, and re-layouts, conv_second(): taken[:, step_f:step_f + 2 * quarter - 1:2]  56.1 us
    all_gather x1, waiting for transfers between devices, on_device(): second_full = lax.all_gather(w_second, ('rec', 'tm'), axis=0, tiled=True)  56.1 us
    dot_general x5, matrix products, add_product(): return jnp.dot(inputs, piece, preferred_element_type=jnp.float32)  31 us
    mul x8, other arithmetic, conv_second(): taken = taken * same_seg[:, None, None]  23.8 us
  transfers between devices with their start and end apart: 11, of which 4 were waited for; matrix products, arithmetic and copies ran while one was open for 86% of the time, Pallas kernels for 0%

commit v1 on v0

--- a/solution.py
+++ b/solution.py
@@ -158,7 +158,12 @@
     bounds = jnp.cumsum(lengths[0])
     local_mel = mel_frames[0]
     first_base = index * frames_dev
-    second_full = lax.all_gather(w_second, ("rec", "tm"), axis=0, tiled=True)
+    second_full = jnp.concatenate(
+        lax.all_to_all(
+            jnp.stack([w_second] * lax.axis_size(("rec", "tm")), axis=0), ("rec", "tm"), 0, 0
+        ),
+        0,
+    )
     block_count = tokens_dev // CONV_BLOCK
     mel_edge = passed_along(local_mel[frames_dev - 3 :], "tm", 1)
     extended = jnp.concatenate([mel_edge, local_mel], axis=0)

time: 886 us -> 840 us (0.948)
  waiting for transfers between devices: 74 us -> 38.3 us
  local copies, waits for them, and re-layouts: 458 us -> 444 us
  starting transfers between devices: 14 us -> 25.8 us
    all_gather x1 -> x0, waiting for transfers between devices: 56.1 us -> none  [on_device(): second_full = lax.all_gather(w_second, ('rec', 'tm'), axis=0, tiled=True)]
    all_to_all x0 -> x1, waiting for transfers between devices: none -> 20.4 us  [on_device(): lax.all_to_all(jnp.stack([w_second] * lax.axis_size(('rec', 'tm')), axis=...]
    all_to_all x0 -> x1, starting transfers between devices: none -> 10.2 us  [on_device(): lax.all_to_all(jnp.stack([w_second] * lax.axis_size(('rec', 'tm')), axis=...]
  transfers between devices with their start and end apart: 11 -> 11, of which waited for: 4 -> 4; matrix products, arithmetic and copies ran while one was open for 86% -> 88% of each run, Pallas kernels for 0% -> 0%
where the time goes in v1:
time: 840 us; the launch traced here: 835 us
  local copies, waits for them, and re-layouts  444 us (53%)
  matrix products  201 us (24%)
  other arithmetic  99.5 us (12%)
  waiting for transfers between devices  38.3 us (5%)
  starting transfers between devices  25.8 us (3%)
  between operations  13.5 us (2%)
  loops' own time  12.7 us (2%)
    slice x72, local copies, waits for them, and re-layouts, conv_second(): taken[:, step_f:step_f + 2 * quarter - 1:2]  284 us
    dot_general x72, matrix products, conv_second(): jnp.dot(columns, w_second[offset:offset + channels], preferred_element_ty...  144 us
    convert_element_type x8, other arithmetic, conv_first(): return jnp.maximum(total, 0.0).astype(jnp.bfloat16)  61.5 us
    slice x72, local copies, waits for them, and re-layouts, conv_first(): columns = taken[:, step_f:step_f + bins - 1:2]  57.2 us
    reshape x72, local copies, waits for them, and re-layouts, conv_second(): taken[:, step_f:step_f + 2 * quarter - 1:2]  55.9 us
    dot_general x5, matrix products, add_product(): return jnp.dot(inputs, piece, preferred_element_type=jnp.float32)  31.1 us
    mul x8, other arithmetic, conv_second(): taken = taken * same_seg[:, None, None]  23.9 us
    all_to_all x1, waiting for transfers between devices, on_device(): lax.all_to_all(jnp.stack([w_second] * lax.axis_size(('rec', 'tm')), axis=...  20.4 us
  transfers between devices with their start and end apart: 11, of which 4 were waited for; matrix products, arithmetic and copies ran while one was open for 88% of the time, Pallas kernels for 0%

profile of v1, /device:TPU:25, one launch (start us, length us, event | category | flops | bytes accessed | tf_op | source)
XLA Modules:
  0.0 834.7 jit_solution(8870315891327239908)
XLA Ops:
  15.9 10.2 %all-to-all-start = ((bf16[128,18,256]{2,1,0:T(8,128)(2,1)}), bf16[128,18,256]{2,1,0:T(8,128)(2,1)S(1)}, u32[]{:S(2)}, u32[]{:S(2)}) async-start(bf16[128,18,256]{2,1,0:T(8,128)(2,1)} %stack.2), calls=%async_computation | async-start | bytes 3145728 | tf_op jit(solution)/shard_map/all_to_all | solution.py:162
  28.4 20.4 %all-to-all-done = bf16[128,18,256]{2,1,0:T(8,128)(2,1)S(1)} async-done(((bf16[128,18,256]{2,1,0:T(8,128)(2,1)}), bf16[128,18,256]{2,1,0:T(8,128)(2,1)S(1)}, u32[]{:S(2)}, u32[]{:S(2)}) %all-to-all-start) | async-done | bytes 1179680 | tf_op jit(solution)/shard_map/all_to_all | solution.py:162
  50.0 667.4 %while.25 = (s32[]{:T(128)}, bf16[8,64,5120]{2,1,0:T(8,128)(2,1)}, s32[8]{0:T(128)S(1)}, bf16[2051,80]{1,0:T(8,128)(2,1)S(1)}, s32[]{:T(128)}, /*index=5*/s32[4]...) while((s32[]{:T(128)}, bf16[8,64,5120]{2,1,0:T(8,128)(2,1)}, ...), condition=%wide.region_3.4_spmd, body=%wide.region_1.3_spmd.sunk | while | flops 1543876352 | bytes 95192408 | solution.py:179
  59.7 7.7 maximum_convert_fusion.2
  71.1 6.9 slice.735
  84.1 4.9 slice.737
  104.4 4.9 slice.740
  124.6 4.9 slice.743
  143.4 7.7 maximum_convert_fusion.2
  154.8 6.9 slice.735
  167.6 4.9 slice.737
  187.8 4.9 slice.740
  208.0 4.9 slice.743
  226.8 7.7 maximum_convert_fusion.2
  238.2 6.9 slice.735
  251.0 4.9 slice.737
  271.3 4.9 slice.740
  291.6 4.9 slice.743
  310.3 7.7 maximum_convert_fusion.2
  321.7 6.9 slice.735
  334.5 4.9 slice.737
  354.7 4.9 slice.740
  374.9 4.9 slice.743
  393.7 7.7 maximum_convert_fusion.2
  405.1 6.9 slice.735
  417.8 4.9 slice.737
  438.1 4.9 slice.740
  458.3 4.9 slice.743
  477.0 7.7 maximum_convert_fusion.2
  488.4 6.9 slice.735
  501.2 4.9 slice.737
  521.5 4.9 slice.740
  541.7 4.9 slice.743
  560.4 7.7 maximum_convert_fusion.2
  571.8 6.9 slice.735
  584.5 4.9 slice.737
  604.8 4.9 slice.740
  625.0 4.9 slice.743
  643.7 7.7 maximum_convert_fusion.2
  655.1 6.9 slice.735
  667.9 4.9 slice.737
  688.2 4.9 slice.740
  717.5 10.0 %fusion.62 = (f32[512]{0:T(512)S(1)}, f32[512,1024]{1,0:T(8,128)S(1)}) fusion(bf16[512,5120]{1,0:T(8,128)(2,1)} %bitcast.117, bf16[5120,1024]{1,0:T(8,128)(2,1)} %all-gather.6.cloned.1.call-done), kind=kOutput, calls=%fused_computation.140 | convolution fusion | flops 5369232896 | bytes 17827840 | tf_op jit(solution)/shard_map/dot_general | solution.py:135
  728.2 6.6 convolution_convert_fusion.1
  734.9 5.6 collective-permute-start.1
  746.7 6.5 collective-permute-done.2
  755.0 46.4 %while.26 = (s32[]{:T(128)}, bf16[8,512,128]{1,2,0:T(8,128)(2,1)}, s32[8]{0:T(128)S(1)}, bf16[512,1024]{1,0:T(8,128)(2,1)S(1)}, bf16[768,2048]{1,0:T(8,128)(2,1)...) while((s32[]{:T(128)}, bf16[8,512,128]{1,2,0:T(8,128)(2,1)}, ...), condition=%wide.region_11.12_spmd.clone, body=%wide.region_8.11_spmd.clone.sunk | while | flops 212401152 | bytes 5925630 | solution.py:116
  820.2 6.0 fusion.64
  (753 shorter events, 514.2 us)
Async XLA Ops:
  6.5 710.9 %all-gather.6.cloned.1.call-start = ((), (), s32[]{:S(2)}) async-start(), calls=%async_computation.1 | async-start | bytes 10567680 | tf_op jit(solution)/shard_map/all_gather | solution.py:181
  7.3 720.6 %all-gather.8.cloned.1.call-start = ((), (), s32[]{:S(2)}) async-start(), calls=%async_computation.2 | async-start | bytes 6340608 | tf_op jit(solution)/shard_map/all_gather | solution.py:187
  8.0 793.4 %all-gather.10.cloned.1.call-start = ((), (), s32[]{:S(2)}) async-start(), calls=%async_computation.3 | async-start | bytes 2113536 | tf_op jit(solution)/shard_map/all_gather | solution.py:196
  8.7 796.9 %all-gather.12.cloned.1.call-start = ((), (), s32[]{:S(2)}) async-start(), calls=%async_computation.4 | async-start | bytes 4227072 | tf_op jit(solution)/shard_map/all_gather | solution.py:199
  10.6 16.1 %copy-start.20 = (s32[1,4]{1,0:T(1,128)S(1)}, s32[1,4]{1,0:T(1,128)}, u32[]{:S(2)}) copy-start(s32[1,4]{1,0:T(1,128)} %param.18) | copy-start | bytes 52
  10.6 17.6 %collective-permute-start = (bf16[3,80]{1,0:T(4,128)(2,1)S(1)}, bf16[3,80]{1,0:T(4,128)(2,1)S(1)}, u32[]{:S(2)}, u32[]{:S(2)}) collective-permute-start(bf16[3,80]{1,0:T(4,128)(2,1)S(1)} %slice_bitcast_fusion), channel_id=1, source_target_pairs={{0,1},{1,2},{2,3},{3,4},{4,5},{5,6},{6,7},{7,8},{8,9},{9,10},{10,1... | collective-permute-start | bytes 1448 | tf_op jit(solution)/shard_map/ppermute | solution.py:18
  15.9 32.9 %all-to-all-start = ((bf16[128,18,256]{2,1,0:T(8,128)(2,1)}), bf16[128,18,256]{2,1,0:T(8,128)(2,1)S(1)}, u32[]{:S(2)}, u32[]{:S(2)}) async-start(bf16[128,18,256]{2,1,0:T(8,128)(2,1)} %stack.2), calls=%async_computation | async-start | bytes 3145728 | tf_op jit(solution)/shard_map/all_to_all | solution.py:162
  26.0 24.0 %copy-start.9 = (f32[3,3,256]{2,1,0:T(4,128)S(1)}, f32[3,3,256]{2,1,0:T(4,128)}, u32[]{:S(2)}) copy-start(f32[3,3,256]{2,1,0:T(4,128)} %param.19) | copy-start | bytes 27652
  26.1 789.8 %all-gather.14.cloned.1.call-start = ((), (), s32[]{:S(2)}) async-start(), calls=%async_computation.5 | async-start | bytes 2113536 | tf_op jit(solution)/shard_map/all_gather | solution.py:206
  50.0 9.7 %copy-start.7 = (bf16[2051,80]{1,0:T(8,128)(2,1)}, bf16[2051,80]{1,0:T(8,128)(2,1)S(1)}, u32[]{:S(2)}) copy-start(bf16[2051,80]{1,0:T(8,128)(2,1)S(1)} %get-tuple-element.446) | copy-start | bytes 984484 | tf_op jit(solution)/shard_map/while
  50.0 9.7 %copy-start.12 = (s32[4]{0:T(128)}, s32[4]{0:T(128)S(1)}, u32[]{:S(2)}) copy-start(s32[4]{0:T(128)S(1)} %get-tuple-element.448) | copy-start | bytes 52 | tf_op jit(solution)/shard_map/while
  92.7 6.0 copy-start.4
  112.9 6.0 copy-start.3
  133.7 9.7 %copy-start.7 = (bf16[2051,80]{1,0:T(8,128)(2,1)}, bf16[2051,80]{1,0:T(8,128)(2,1)S(1)}, u32[]{:S(2)}) copy-start(bf16[2051,80]{1,0:T(8,128)(2,1)S(1)} %get-tuple-element.446) | copy-start | bytes 984484 | tf_op jit(solution)/shard_map/while
  133.7 9.7 %copy-start.12 = (s32[4]{0:T(128)}, s32[4]{0:T(128)S(1)}, u32[]{:S(2)}) copy-start(s32[4]{0:T(128)S(1)} %get-tuple-element.448) | copy-start | bytes 52 | tf_op jit(solution)/shard_map/while
  176.1 6.0 copy-start.4
  196.4 6.0 copy-start.3
  217.1 9.7 %copy-start.7 = (bf16[2051,80]{1,0:T(8,128)(2,1)}, bf16[2051,80]{1,0:T(8,128)(2,1)S(1)}, u32[]{:S(2)}) copy-start(bf16[2051,80]{1,0:T(8,128)(2,1)S(1)} %get-tuple-element.446) | copy-start | bytes 984484 | tf_op jit(solution)/shard_map/while
  217.2 9.7 %copy-start.12 = (s32[4]{0:T(128)}, s32[4]{0:T(128)S(1)}, u32[]{:S(2)}) copy-start(s32[4]{0:T(128)S(1)} %get-tuple-element.448) | copy-start | bytes 52 | tf_op jit(solution)/shard_map/while
  259.6 6.0 copy-start.4
  279.8 6.1 copy-start.3
  300.6 9.7 %copy-start.7 = (bf16[2051,80]{1,0:T(8,128)(2,1)}, bf16[2051,80]{1,0:T(8,128)(2,1)S(1)}, u32[]{:S(2)}) copy-start(bf16[2051,80]{1,0:T(8,128)(2,1)S(1)} %get-tuple-element.446) | copy-start | bytes 984484 | tf_op jit(solution)/shard_map/while
  300.6 9.7 %copy-start.12 = (s32[4]{0:T(128)}, s32[4]{0:T(128)S(1)}, u32[]{:S(2)}) copy-start(s32[4]{0:T(128)S(1)} %get-tuple-element.448) | copy-start | bytes 52 | tf_op jit(solution)/shard_map/while
  343.0 6.0 copy-start.4
  363.3 6.0 copy-start.3
  384.0 9.7 %copy-start.7 = (bf16[2051,80]{1,0:T(8,128)(2,1)}, bf16[2051,80]{1,0:T(8,128)(2,1)S(1)}, u32[]{:S(2)}) copy-start(bf16[2051,80]{1,0:T(8,128)(2,1)S(1)} %get-tuple-element.446) | copy-start | bytes 984484 | tf_op jit(solution)/shard_map/while
  384.0 9.7 %copy-start.12 = (s32[4]{0:T(128)}, s32[4]{0:T(128)S(1)}, u32[]{:S(2)}) copy-start(s32[4]{0:T(128)S(1)} %get-tuple-element.448) | copy-start | bytes 52 | tf_op jit(solution)/shard_map/while
  426.4 6.0 copy-start.4
  467.3 9.7 %copy-start.7 = (bf16[2051,80]{1,0:T(8,128)(2,1)}, bf16[2051,80]{1,0:T(8,128)(2,1)S(1)}, u32[]{:S(2)}) copy-start(bf16[2051,80]{1,0:T(8,128)(2,1)S(1)} %get-tuple-element.446) | copy-start | bytes 984484 | tf_op jit(solution)/shard_map/while
  467.3 9.7 %copy-start.12 = (s32[4]{0:T(128)}, s32[4]{0:T(128)S(1)}, u32[]{:S(2)}) copy-start(s32[4]{0:T(128)S(1)} %get-tuple-element.448) | copy-start | bytes 52 | tf_op jit(solution)/shard_map/while
  509.8 6.0 copy-start.4
  550.7 9.7 %copy-start.7 = (bf16[2051,80]{1,0:T(8,128)(2,1)}, bf16[2051,80]{1,0:T(8,128)(2,1)S(1)}, u32[]{:S(2)}) copy-start(bf16[2051,80]{1,0:T(8,128)(2,1)S(1)} %get-tuple-element.446) | copy-start | bytes 984484 | tf_op jit(solution)/shard_map/while
  550.7 9.7 %copy-start.12 = (s32[4]{0:T(128)}, s32[4]{0:T(128)S(1)}, u32[]{:S(2)}) copy-start(s32[4]{0:T(128)S(1)} %get-tuple-element.448) | copy-start | bytes 52 | tf_op jit(solution)/shard_map/while
  593.1 6.0 copy-start.4
  634.0 9.7 %copy-start.7 = (bf16[2051,80]{1,0:T(8,128)(2,1)}, bf16[2051,80]{1,0:T(8,128)(2,1)S(1)}, u32[]{:S(2)}) copy-start(bf16[2051,80]{1,0:T(8,128)(2,1)S(1)} %get-tuple-element.446) | copy-start | bytes 984484 | tf_op jit(solution)/shard_map/while
  634.1 9.7 %copy-start.12 = (s32[4]{0:T(128)}, s32[4]{0:T(128)S(1)}, u32[]{:S(2)}) copy-start(s32[4]{0:T(128)S(1)} %get-tuple-element.448) | copy-start | bytes 52 | tf_op jit(solution)/shard_map/while
  676.5 6.0 copy-start.4
  727.5 7.3 copy-start.6
  734.8 8.1 copy-start.5
  734.8 7.7 copy-start.14
  734.8 7.7 copy-start.16
  734.8 7.8 copy-start.10
  734.8 7.8 copy-start.11
  734.9 11.7 %collective-permute-start.1 = (bf16[128,2048]{1,0:T(8,128)(2,1)S(1)}, bf16[128,2048]{1,0:T(8,128)(2,1)S(1)}, u32[]{:S(2)}, u32[]{:S(2)}) collective-permute-start(bf16[128,2048]{1,0:T(8,128)(2,1)S(1)} %get-tuple-element.258), channel_id=1, source_target_pairs={{0,1},{1,2},{2,3},{3,4},{4,5},{5,6},{6,7},{7,8},{8,9},{9,10},{10,1... | collective-permute-start | bytes 1572872 | tf_op jit(solution)/shard_map/ppermute | solution.py:26
  740.6 12.6 %collective-permute-start.2 = (bf16[128,2048]{1,0:T(8,128)(2,1)S(1)}, bf16[128,2048]{1,0:T(8,128)(2,1)S(1)}, u32[]{:S(2)}, u32[]{:S(2)}) collective-permute-start(bf16[128,2048]{1,0:T(8,128)(2,1)S(1)} %get-tuple-element.259), channel_id=1, source_target_pairs={{1,0},{2,1},{3,2},{4,3},{5,4},{6,5},{7,6},{8,7},{9,8},{10,9},{11,1... | collective-permute-start | bytes 1572872 | tf_op jit(solution)/shard_map/ppermute | solution.py:29
  742.9 12.1 %slice-start = ((bf16[512,3072]{1,0:T(8,128)(2,1)}), bf16[512,1024]{1,0:T(8,128)(2,1)S(1)}, s32[]{:S(2)}) async-start(bf16[512,3072]{1,0:T(8,128)(2,1)} %copy-done.5), calls=%async_computation.6 | async-start | bytes 2097152 | tf_op jit(solution)/shard_map/slice | solution.py:190
  811.2 4.7 collective-permute-start.3
  813.1 7.1 collective-permute-start.4
  (64 other events, 157.1 us)
Sparse Core Ops, SparseCore 0:
  10.5 83.6 all-gather.5
  97.3 65.5 all-gather.7
  166.0 62.7 all-gather.9
  231.8 64.3 all-gather.11
  299.1 62.7 all-gather.13
